TPU v7x, 32 devices: a whole 2x2x4 slice. The times are simulated.
32 devices in a mesh: ctx: 8 (over z, x), fsdp: 4 (over y, core).
Axes of the slice: x: 2, y: 2, z: 4, core: 2. Of those that a mesh axis runs over, the one named last changes fastest.
Arguments:
- layer_input: bfloat16 [4096, 1024], P(('ctx', 'fsdp')), may hold values from -40 to 40, as said below
- gain_attn: bfloat16 [1024], P('fsdp'), may hold values from 0.25 to 1.75
- w_qkv: bfloat16 [1024, 3072], P('fsdp'), may hold values from -1 to 1
- w_out: bfloat16 [1024, 1024], P('fsdp'), may hold values from -3.5 to 3.5
- gain_mlp: bfloat16 [1024], P('fsdp'), may hold values from 0.25 to 1.75
- w_in: bfloat16 [1024, 5248], P('fsdp'), may hold values from -0.1875 to 0.1875
- w_down: bfloat16 [2624, 1024], P('fsdp'), may hold values from -0.125 to 0.125
- cotangent: bfloat16 [4096, 1024], P(('ctx', 'fsdp')), may hold values from -36 to 36
Outputs:
- layer_output: bfloat16 [4096, 1024], P(('ctx', 'fsdp'))
- d_x: float32 [4096, 1024], P(('ctx', 'fsdp'))
- d_gain_attn: float32 [1024], P('fsdp')
- d_gain_mlp: float32 [1024], P('fsdp')
- d_w_qkv: float32 [1024, 3072], P('fsdp')
- d_w_out: float32 [1024, 1024], P('fsdp')
- d_w_in: float32 [1024, 5248], P('fsdp')
- d_w_down: float32 [2624, 1024], P('fsdp')
Inputs may be any that keep to these rules, and one draw needn't show every extreme that they name: `layer_input`: input activations with feature scales and token scales that differ.
All inputs are finite; a program needn't handle non-finite values.
Results may differ from a plain program's by a relative error of at most 0.019.
Values may be sent and summed in bfloat16 or wider, within the bound.
No kernel may reach another device: no remote copies, remote signals or barrier semaphores. Data moves between devices by JAX's collectives and lax.ppermute only.
A program may use at most 448 MiB of HBM per device.

v0:
```python
import math
import jax
import jax.numpy as jnp
from jax import lax
from jax.sharding import PartitionSpec as P

H = 16
HD = 64
EPS = 1e-05
THETA = 160000.0
SQRT_HALF = 0.7071067811865476
INV_SQRT_TAU = 0.3989422804014327


def layer_norm(values, gain):
    middle = jnp.mean(values, axis=-1, keepdims=True)
    centered = values - middle
    spread = jnp.mean(centered * centered, axis=-1, keepdims=True)
    inverse = lax.rsqrt(spread + EPS)
    normed = centered * inverse
    return (normed * gain, normed, inverse)


def norm_back(incoming, normed, inverse, gain):
    scaled = incoming * gain
    return inverse * (
        scaled
        - jnp.mean(scaled, axis=-1, keepdims=True)
        - normed * jnp.mean(scaled * normed, axis=-1, keepdims=True)
    )


def rope_tables(positions, width):
    half = width // 2
    freq = THETA ** (-(jnp.arange(half).astype(jnp.float32) * 2.0 / width))
    angle = positions[:, None] * freq[None, :]
    return (jnp.cos(angle), jnp.sin(angle))


def rotate(values, cosine, sine, sign):
    half = values.shape[-1] // 2
    first = values[..., :half]
    second = values[..., half:]
    cos_b = cosine[:, None, :]
    sin_b = sine[:, None, :] * sign
    return jnp.concatenate(
        [first * cos_b - second * sin_b, second * cos_b + first * sin_b], axis=-1
    )


def gelu_value(inner):
    return 0.5 * inner * (1.0 + lax.erf(inner * SQRT_HALF))


def gelu_slope(inner):
    return (
        0.5 * (1.0 + lax.erf(inner * SQRT_HALF))
        + inner * jnp.exp(-0.5 * inner * inner) * INV_SQRT_TAU
    )


def front_dot(left, right):
    return lax.dot_general(
        left, right, (((0,), (0,)), ((), ())), preferred_element_type=jnp.float32
    )


def back_dot(left, right):
    return lax.dot_general(
        left, right, (((1,), (1,)), ((), ())), preferred_element_type=jnp.float32
    )


def attend(queries, keys, values):
    total = keys.shape[0]
    step = math.gcd(total, 1024)
    rows, heads, width = queries.shape

    def measure(carry, index):
        top, mass = carry
        key_blk = lax.dynamic_slice_in_dim(keys, index * step, step, 0)
        score = (
            jnp.einsum("qhd,khd->hqk", queries, key_blk, preferred_element_type=jnp.float32) * 0.125
        )
        new_top = jnp.maximum(top, jnp.max(score, axis=-1))
        mass = mass * jnp.exp(top - new_top) + jnp.sum(jnp.exp(score - new_top[..., None]), axis=-1)
        return ((new_top, mass), None)

    start = (jnp.full((heads, rows), -jnp.inf, jnp.float32), jnp.zeros((heads, rows), jnp.float32))
    (top, mass), _ = lax.scan(measure, start, jnp.arange(total // step))
    lse = top + jnp.log(mass)

    def gather_values(acc, index):
        key_blk = lax.dynamic_slice_in_dim(keys, index * step, step, 0)
        val_blk = lax.dynamic_slice_in_dim(values, index * step, step, 0)
        score = (
            jnp.einsum("qhd,khd->hqk", queries, key_blk, preferred_element_type=jnp.float32) * 0.125
        )
        probs = jnp.exp(score - lse[..., None]).astype(jnp.bfloat16)
        return (
            acc + jnp.einsum("hqk,khd->hqd", probs, val_blk, preferred_element_type=jnp.float32),
            None,
        )

    acc, _ = lax.scan(
        gather_values, jnp.zeros((heads, rows, width), jnp.float32), jnp.arange(total // step)
    )
    result = acc.astype(jnp.bfloat16).transpose(1, 0, 2)
    return (result, lse)


def key_terms(queries, grads, lse, delta, key_blk, val_blk):
    score = jnp.einsum("qhd,khd->hqk", queries, key_blk, preferred_element_type=jnp.float32) * 0.125
    probs = jnp.exp(score - lse[..., None])
    d_probs = jnp.einsum("qhd,khd->hqk", grads, val_blk, preferred_element_type=jnp.float32)
    d_score = (probs * (d_probs - delta[..., None])).astype(jnp.bfloat16)
    d_key = jnp.einsum("hqk,qhd->khd", d_score, queries, preferred_element_type=jnp.float32) * 0.125
    d_value = jnp.einsum(
        "hqk,qhd->khd", probs.astype(jnp.bfloat16), grads, preferred_element_type=jnp.float32
    )
    return (d_key, d_value)


def attend_back(queries, keys, values, grads, lse, delta):
    total = keys.shape[0]
    step = math.gcd(total, 1024)
    rows, heads, width = queries.shape

    def attend_advance(d_query, index):
        key_blk = lax.dynamic_slice_in_dim(keys, index * step, step, 0)
        val_blk = lax.dynamic_slice_in_dim(values, index * step, step, 0)
        score = (
            jnp.einsum("qhd,khd->hqk", queries, key_blk, preferred_element_type=jnp.float32) * 0.125
        )
        probs = jnp.exp(score - lse[..., None])
        d_probs = jnp.einsum("qhd,khd->hqk", grads, val_blk, preferred_element_type=jnp.float32)
        d_score = (probs * (d_probs - delta[..., None])).astype(jnp.bfloat16)
        d_query = (
            d_query
            + jnp.einsum("hqk,khd->qhd", d_score, key_blk, preferred_element_type=jnp.float32)
            * 0.125
        )
        return (d_query, None)

    d_query, _ = lax.scan(
        attend_advance, jnp.zeros((rows, heads, width), jnp.float32), jnp.arange(total // step)
    )
    return d_query


def owner_fold(stats, own_keys, own_values):

    def fold(carry, piece, start):
        query_rows, grad_rows = piece
        count = query_rows.shape[0]
        step = math.gcd(count, 512)

        def fold_advance(acc, index):
            offset = index * step
            q_blk = lax.dynamic_slice_in_dim(query_rows, offset, step, 0)
            g_blk = lax.dynamic_slice_in_dim(grad_rows, offset, step, 0)
            lse_blk = lax.dynamic_slice_in_dim(stats[0], offset, step, 0)
            delta_blk = lax.dynamic_slice_in_dim(stats[1], offset, step, 0)
            d_key, d_value = key_terms(q_blk, g_blk, lse_blk.T, delta_blk.T, own_keys, own_values)
            return ((acc[0] + d_key, acc[1] + d_value), None)

        result, _ = lax.scan(fold_advance, carry, jnp.arange(count // step))
        return result

    return fold


def on_device(layer_input, gain_attn, w_qkv, w_out, gain_mlp, w_in, w_down, cotangent):
    whole = (
        lax.all_gather(gain_attn, "fsdp", axis=0, tiled=True),
        lax.all_gather(w_qkv, "fsdp", axis=0, tiled=True),
        lax.all_gather(w_out, "fsdp", axis=0, tiled=True),
        lax.all_gather(gain_mlp, "fsdp", axis=0, tiled=True),
        lax.all_gather(w_in, "fsdp", axis=0, tiled=True),
        lax.all_gather(w_down, "fsdp", axis=0, tiled=True),
    )
    gain_one = whole[0].astype(jnp.float32)
    qkv_full = whole[1]
    out_full = whole[2]
    gain_two = whole[3].astype(jnp.float32)
    in_full = whole[4]
    down_full = whole[5]
    rows, width = layer_input.shape
    groups = lax.axis_size("fsdp")
    block = rows * groups
    first_row = lax.axis_index("ctx") * block + lax.axis_index("fsdp") * rows
    xf = layer_input.astype(jnp.float32)
    xn1, n1, r1 = layer_norm(xf, gain_one)
    xn1b = xn1.astype(jnp.bfloat16)
    qkv = jnp.dot(xn1b, qkv_full, preferred_element_type=jnp.float32).reshape(rows, 3, H, HD)
    positions = (first_row + jnp.arange(rows)).astype(jnp.float32)
    cosine, sine = rope_tables(positions, HD)
    queries = rotate(qkv[:, 0], cosine, sine, 1.0).astype(jnp.bfloat16)
    keys = rotate(qkv[:, 1], cosine, sine, 1.0).astype(jnp.bfloat16)
    values = qkv[:, 2].astype(jnp.bfloat16)
    all_keys, all_values = (
        lax.all_gather(keys.reshape(rows, width), ("ctx", "fsdp"), axis=0, tiled=True),
        lax.all_gather(values.reshape(rows, width), ("ctx", "fsdp"), axis=0, tiled=True),
    )
    all_keys = all_keys.reshape(-1, H, HD)
    all_values = all_values.reshape(-1, H, HD)
    o_here, lse = attend(queries, all_keys, all_values)
    attended = o_here.reshape(rows, width)
    hidden = xf + jnp.dot(attended, out_full, preferred_element_type=jnp.float32)
    xn2, n2, r2 = layer_norm(hidden, gain_two)
    xn2b = xn2.astype(jnp.bfloat16)
    both = jnp.dot(xn2b, in_full, preferred_element_type=jnp.float32)
    ff_width = both.shape[1] // 2
    act_in = both[:, :ff_width]
    gate_in = both[:, ff_width:]
    mixed = (gelu_value(act_in) * gate_in).astype(jnp.bfloat16)
    output = (hidden + jnp.dot(mixed, down_full, preferred_element_type=jnp.float32)).astype(
        jnp.bfloat16
    )
    grad_f = cotangent.astype(jnp.float32)
    d_w_down = front_dot(mixed, cotangent)
    d_mixed = back_dot(cotangent, down_full)
    d_both = jnp.concatenate(
        [d_mixed * gate_in * gelu_slope(act_in), d_mixed * gelu_value(act_in)], axis=1
    ).astype(jnp.bfloat16)
    d_w_in = front_dot(xn2b, d_both)
    d_xn2 = back_dot(d_both, in_full)
    d_gain_mlp = jnp.sum(d_xn2 * n2, axis=0)
    d_hidden = grad_f + norm_back(d_xn2, n2, r2, gain_two)
    d_hidden_b = d_hidden.astype(jnp.bfloat16)
    d_w_out = front_dot(attended, d_hidden_b)
    d_attended = back_dot(d_hidden_b, out_full).astype(jnp.bfloat16)
    grads_here = d_attended.reshape(rows, H, HD)
    delta = jnp.sum(grads_here.astype(jnp.float32) * o_here.astype(jnp.float32), axis=-1).T
    d_query = attend_back(queries, all_keys, all_values, grads_here, lse, delta)
    stats = (
        lax.all_gather(lse.T, ("ctx", "fsdp"), axis=0, tiled=True),
        lax.all_gather(delta.T, ("ctx", "fsdp"), axis=0, tiled=True),
    )
    empty = jnp.zeros((rows, H, HD), jnp.float32)
    fold = owner_fold(stats, keys, values)
    d_key, d_value = fold(
        (empty, empty),
        (
            lax.all_gather(queries, ("ctx", "fsdp"), axis=0, tiled=True),
            lax.all_gather(grads_here, ("ctx", "fsdp"), axis=0, tiled=True),
        ),
        jnp.int32(0),
    )
    query_back = rotate(d_query, cosine, sine, -1.0).reshape(rows, width)
    key_back = rotate(d_key, cosine, sine, -1.0).reshape(rows, width)
    d_qkv = jnp.concatenate([query_back, key_back, d_value.reshape(rows, width)], axis=1).astype(
        jnp.bfloat16
    )
    d_w_qkv = front_dot(xn1b, d_qkv)
    d_xn1 = back_dot(d_qkv, qkv_full)
    d_gain_attn = jnp.sum(d_xn1 * n1, axis=0)
    d_x = d_hidden + norm_back(d_xn1, n1, r1, gain_one)
    shards = (
        lax.psum_scatter(
            d_gain_attn.astype(jnp.bfloat16), "fsdp", scatter_dimension=0, tiled=True
        ).astype(jnp.float32),
        lax.psum_scatter(
            d_w_qkv.astype(jnp.bfloat16), "fsdp", scatter_dimension=0, tiled=True
        ).astype(jnp.float32),
        lax.psum_scatter(
            d_w_out.astype(jnp.bfloat16), "fsdp", scatter_dimension=0, tiled=True
        ).astype(jnp.float32),
        lax.psum_scatter(
            d_gain_mlp.astype(jnp.bfloat16), "fsdp", scatter_dimension=0, tiled=True
        ).astype(jnp.float32),
        lax.psum_scatter(
            d_w_in.astype(jnp.bfloat16), "fsdp", scatter_dimension=0, tiled=True
        ).astype(jnp.float32),
        lax.psum_scatter(
            d_w_down.astype(jnp.bfloat16), "fsdp", scatter_dimension=0, tiled=True
        ).astype(jnp.float32),
    )
    summed = (
        lax.psum(shards[0].astype(jnp.bfloat16), "ctx").astype(jnp.float32),
        lax.psum(shards[1].astype(jnp.bfloat16), "ctx").astype(jnp.float32),
        lax.psum(shards[2].astype(jnp.bfloat16), "ctx").astype(jnp.float32),
        lax.psum(shards[3].astype(jnp.bfloat16), "ctx").astype(jnp.float32),
        lax.psum(shards[4].astype(jnp.bfloat16), "ctx").astype(jnp.float32),
        lax.psum(shards[5].astype(jnp.bfloat16), "ctx").astype(jnp.float32),
    )
    return (output, d_x, summed[0], summed[3], summed[1], summed[2], summed[4], summed[5])


def solution(mesh):
    return jax.shard_map(
        on_device,
        mesh=mesh,
        in_specs=(
            P(("ctx", "fsdp"), None),
            P("fsdp"),
            P("fsdp", None),
            P("fsdp", None),
            P("fsdp"),
            P("fsdp", None),
            P("fsdp", None),
            P(("ctx", "fsdp"), None),
        ),
        out_specs=(
            P(("ctx", "fsdp"), None),
            P(("ctx", "fsdp"), None),
            P("fsdp"),
            P("fsdp"),
            P("fsdp", None),
            P("fsdp", None),
            P("fsdp", None),
            P("fsdp", None),
        ),
        check_vma=False,
    )
```

profile of v0, /device:TPU:0, one launch (start us, length us, event | category | flops | bytes accessed | tf_op | source)
XLA Modules:
  0.0 1043.8 jit_solution(7189719437564355029)
XLA Ops:
  17.1 41.7 %all-gather.11.cloned.1.call-done = bf16[1024,3072]{1,0:T(8,128)(2,1)} async-done(((bf16[256,3072]{1,0:T(8,128)(2,1)}), bf16[1024,3072]{1,0:T(8,128)(2,1)}) %all-gather.11.cloned.1.call-update) | async-done | bytes 6291472 | tf_op jit(solution)/shard_map/all_gather | solution.py:176
  74.0 83.3 %all-gather.13.cloned.1.call-done = bf16[4096,1024]{0,1:T(8,128)(2,1)} async-done(((bf16[128,1024]{0,1:T(8,128)(2,1)}), bf16[4096,1024]{0,1:T(8,128)(2,1)}) %all-gather.13.cloned.1.call-update) | async-done | bytes 8388624 | tf_op jit(solution)/shard_map/all_gather | solution.py:202
  157.3 50.1 %while.48 = (s32[]{:T(128)}, f32[16,128]{1,0:T(8,128)S(1)}, f32[16,128]{1,0:T(8,128)S(1)}, s32[4]{0:T(128)S(1)}, bf16[4096,16,64]{0,2,1:T(8,128)(2,1)}, /*index=...) while((s32[]{:T(128)}, f32[16,128]{1,0:T(8,128)S(1)}, ...), condition=%wide.region_5.6_spmd.clone, body=%wide.region_2.5_spmd.clone.sunk | while | flops 278931456 | bytes 19243188 | solution.py:90
  196.2 6.4 bitcast_reduce_fusion.2
  207.4 43.3 %all-gather.15.cloned.1.call-done = bf16[4096,1024]{0,1:T(8,128)(2,1)} async-done(((bf16[128,1024]{0,1:T(8,128)(2,1)}), bf16[4096,1024]{0,1:T(8,128)(2,1)}) %all-gather.15.cloned.1.call-update) | async-done | bytes 8388624 | tf_op jit(solution)/shard_map/all_gather | solution.py:203
  250.7 25.5 %while.49 = (s32[]{:T(128)}, f32[16,128,64]{1,2,0:T(8,128)S(1)}, s32[4]{0:T(128)S(1)}, bf16[4096,16,64]{0,2,1:T(8,128)(2,1)}, bf16[128,16,64]{0,2,1:T(8,128)(2,1...) while((s32[]{:T(128)}, f32[16,128,64]{1,2,0:T(8,128)S(1)}, ...), condition=%wide.region_7.8_spmd.clone, body=%wide.region_6.7_spmd.clone.sunk | while | flops 543424512 | bytes 5514936 | solution.py:105
  278.6 67.3 %all-gather.19.cloned.1.call-done = bf16[1024,5248]{1,0:T(8,128)(2,1)} async-done(((bf16[256,5248]{1,0:T(8,128)(2,1)}), bf16[1024,5248]{1,0:T(8,128)(2,1)}) %all-gather.19.cloned.1.call-update) | async-done | bytes 10747920 | tf_op jit(solution)/shard_map/all_gather | solution.py:179
  346.0 7.3 fusion.107
  353.2 35.3 %all-gather.21.cloned.1.call-done = bf16[2624,1024]{1,0:T(8,128)(2,1)} async-done(((bf16[656,1024]{1,0:T(8,128)(2,1)}), bf16[2624,1024]{1,0:T(8,128)(2,1)}) %all-gather.21.cloned.1.call-update) | async-done | bytes 5373968 | tf_op jit(solution)/shard_map/all_gather | solution.py:180
  393.9 8.3 multiply_reduce_fusion
  413.4 7.0 convolution_convert_fusion
  422.3 42.8 %all_gather.45 = f32[4096,16]{0,1:T(8,128)S(1)} all-gather(f32[128,16]{0,1:T(8,128)S(1)} %bitcast.127), channel_id=1, replica_groups=mesh['ctx'=8,'fsdp'=4] {'ctx','fsdp'}, dimensions={0}, use_global_device_ids=true | all-gather | bytes 270336 | tf_op jit(solution)/shard_map/all_gather | solution.py:237
  465.3 38.5 %all_gather.47 = f32[4096,16]{0,1:T(8,128)S(1)} all-gather(f32[128,16]{0,1:T(8,128)S(1)} %multiply_reduce_fusion.1), channel_id=1, replica_groups=mesh['ctx'=8,'fsdp'=4] {'ctx','fsdp'}, dimensions={0}, use_global_device_ids=true | all-gather | bytes 270336 | tf_op jit(solution)/shard_map/all_gather | solution.py:238
  503.7 65.3 %while.50 = (s32[]{:T(128)}, f32[128,16,64]{0,2,1:T(8,128)}, s32[4]{0:T(128)S(1)}, bf16[4096,16,64]{0,2,1:T(8,128)(2,1)}, bf16[128,16,64]{0,2,1:T(8,128)(2,1)S(1...) while((s32[]{:T(128)}, f32[128,16,64]{0,2,1:T(8,128)}, ...), condition=%wide.region_14.15_spmd.clone, body=%wide.region_13.14_spmd.clone.sunk | while | flops 816185344 | bytes 24659660 | solution.py:145
  511.3 8.6 fusion.164
  527.4 8.6 fusion.164
  543.7 8.8 fusion.164
  560.0 9.0 fusion.164
  569.0 8.7 all-gather.25.cloned.1.call-done
  577.7 129.6 %while.51 = (s32[]{:T(128)}, f32[128,16,64]{0,2,1:T(8,128)}, f32[128,16,64]{0,2,1:T(8,128)S(1)}, s32[8]{0:T(128)S(1)}, bf16[4096,16,64]{0,2,1:T(8,128)(2,1)}, /*...) while((s32[]{:T(128)}, f32[128,16,64]{0,2,1:T(8,128)}, ...), condition=%wide.region_16.17_spmd.clone, body=%wide.region_15.16_spmd.clone.sunk | while | flops 545914880 | bytes 19629788 | solution.py:167
  583.0 7.1 fusion.173
  599.0 6.8 fusion.173
  614.5 6.7 fusion.173
  631.1 7.6 fusion.173
  647.5 6.7 fusion.173
  662.9 6.8 fusion.173
  679.4 8.7 fusion.173
  697.0 6.7 fusion.173
  713.6 40.5 %reduce-scatter.9.cloned.1.call-done = bf16[256,5248]{1,0:T(8,128)(2,1)} async-done(((bf16[1024,5248]{1,0:T(8,128)(2,1)}), bf16[256,5248]{1,0:T(8,128)(2,1)}) %reduce-scatter.9.cloned.1.call-update) | async-done | bytes 2686992 | tf_op jit(solution)/shard_map/reduce_scatter | solution.py:272
  754.0 61.3 %reduce-scatter.5.cloned.1.call-done = bf16[256,3072]{1,0:T(8,128)(2,1)} async-done(((bf16[1024,3072]{1,0:T(8,128)(2,1)}), bf16[256,3072]{1,0:T(8,128)(2,1)}) %reduce-scatter.5.cloned.1.call-update) | async-done | bytes 1572880 | tf_op jit(solution)/shard_map/reduce_scatter | solution.py:263
  833.7 22.5 %all-reduce.2 = (bf16[256]{0:T(256)(128)(2,1)S(1)}, bf16[256]{0:T(256)(128)(2,1)S(1)}) all-reduce(bf16[256]{0:T(256)(128)(2,1)S(1)} %dynamic-slice.1, bf16[256]{0:T(256)(128)(2,1)S(1)} %dynamic-slice.3), channel_id=1, replica_groups=mesh['ctx'=8,'fsdp'=4] {'ctx'}, use_global_device_ids=true, to_apply=%region_21.22 | all-reduce | flops 512 | bytes 2048 | tf_op jit(solution)/shard_map/psum | solution.py:280
  858.3 169.4 %all-reduce.7.cloned.1.call-done = (bf16[256,3072]{1,0:T(8,128)(2,1)}, bf16[256,1024]{1,0:T(8,128)(2,1)}, bf16[256,5248]{1,0:T(8,128)(2,1)}, bf16[656,1024]{1,0:T(8,128)(2,1)}) async-done(((bf16[256,3072]{1,0:T(8,128)(2,1)}, bf16[256,1024]{1,0:T(8,128)(2,1)}, bf16[256,5248]{1,0:T(8,128)(2,1)}, bf16[656,1024]{1,0:T(8,128)(2,1)}), (bf16[256,3072]{1,0:T(8,128)(2,1)}, bf16[256,1024]{1,0:T(8,128)(2,1)}, ...) | async-done | bytes 6127632 | tf_op jit(solution)/shard_map/psum | solution.py:281
  (198 shorter events, 239.2 us)
Async XLA Ops:
  7.2 51.6 %all-gather.11.cloned.1.call-start = ((), (), s32[]{:S(2)}) async-start(), calls=%async_computation.4 | async-start | bytes 7864320 | tf_op jit(solution)/shard_map/all_gather | solution.py:176
  7.9 149.4 %all-gather.13.cloned.1.call-start = ((), (), s32[]{:S(2)}) async-start(), calls=%async_computation.5 | async-start | bytes 8650752 | tf_op jit(solution)/shard_map/all_gather | solution.py:202
  64.2 3.2 copy-start.4
  65.4 185.3 %all-gather.15.cloned.1.call-start = ((), (), s32[]{:S(2)}) async-start(), calls=%async_computation.6 | async-start | bytes 8650752 | tf_op jit(solution)/shard_map/all_gather | solution.py:203
  66.2 210.0 %all-gather.17.cloned.1.call-start = ((), (), s32[]{:S(2)}) async-start(), calls=%async_computation.7 | async-start | bytes 2621440 | tf_op jit(solution)/shard_map/all_gather | solution.py:177
  66.8 2.1 copy-start.14
  66.8 279.2 %all-gather.19.cloned.1.call-start = ((), (), s32[]{:S(2)}) async-start(), calls=%async_computation.8 | async-start | bytes 13434880 | tf_op jit(solution)/shard_map/all_gather | solution.py:179
  67.4 321.2 %all-gather.21.cloned.1.call-start = ((), (), s32[]{:S(2)}) async-start(), calls=%async_computation.9 | async-start | bytes 6717440 | tf_op jit(solution)/shard_map/all_gather | solution.py:180
  68.0 501.0 %all-gather.23.cloned.1.call-start = ((), (), s32[]{:S(2)}) async-start(), calls=%async_computation.10 | async-start | bytes 8650752 | tf_op jit(solution)/shard_map/all_gather | solution.py:245
  68.9 508.8 %all-gather.25.cloned.1.call-start = ((), (), s32[]{:S(2)}) async-start(), calls=%async_computation.11 | async-start | bytes 8650752 | tf_op jit(solution)/shard_map/all_gather | solution.py:246
  250.7 25.6 %copy-start.2 = (bf16[128,1024]{1,0:T(8,128)(2,1)S(1)}, bf16[128,1024]{1,0:T(8,128)(2,1)}, u32[]{:S(2)}) copy-start(bf16[128,1024]{1,0:T(8,128)(2,1)} %param.16) | copy-start | bytes 786436
  346.0 42.6 %copy-start.8 = (bf16[128,1024]{1,0:T(8,128)(2,1)S(1)}, bf16[128,1024]{1,0:T(8,128)(2,1)}, u32[]{:S(2)}) copy-start(bf16[128,1024]{1,0:T(8,128)(2,1)} %param.23) | copy-start | bytes 786436
  393.9 8.3 copy-start.9
  393.9 8.3 copy-start.11
  393.9 8.6 copy-start.3
  404.2 309.3 %reduce-scatter.7.cloned.1.call-start = ((), (), s32[]{:S(2)}) async-start(), calls=%async_computation.13 | async-start | bytes 2621440 | tf_op jit(solution)/shard_map/reduce_scatter | solution.py:266
  406.3 307.3 %reduce-scatter.11.cloned.1.call-start = ((), (), s32[]{:S(2)}) async-start(), calls=%async_computation.15 | async-start | bytes 6717440 | tf_op jit(solution)/shard_map/reduce_scatter | solution.py:275
  412.3 1.1 copy-start.10
  412.3 341.7 %reduce-scatter.9.cloned.1.call-start = ((), (), s32[]{:S(2)}) async-start(), calls=%async_computation.14 | async-start | bytes 13434880 | tf_op jit(solution)/shard_map/reduce_scatter | solution.py:272
  420.4 44.8 %copy-start.6 = (bf16[128,1024]{0,1:T(8,128)(2,1)S(1)}, bf16[128,1024]{0,1:T(8,128)(2,1)}, u32[]{:S(2)}) copy-start(bf16[128,1024]{0,1:T(8,128)(2,1)} %copy.40) | copy-start | bytes 786436
  420.4 83.3 %copy-start = (bf16[128,16,64]{0,2,1:T(8,128)(2,1)S(1)}, bf16[128,16,64]{0,2,1:T(8,128)(2,1)}, u32[]{:S(2)}) copy-start(bf16[128,16,64]{0,2,1:T(8,128)(2,1)} %get-tuple-element.819) | copy-start | bytes 786436
  420.4 394.9 %reduce-scatter.5.cloned.1.call-start = ((), (), s32[]{:S(2)}) async-start(), calls=%async_computation.12 | async-start | bytes 7864320 | tf_op jit(solution)/shard_map/reduce_scatter | solution.py:263
  503.7 74.0 %copy-start.1 = (bf16[128,16,64]{0,2,1:T(8,128)(2,1)S(1)}, bf16[128,16,64]{0,2,1:T(8,128)(2,1)}, u32[]{:S(2)}) copy-start(bf16[128,16,64]{0,2,1:T(8,128)(2,1)} %maximum_convert_fusion) | copy-start | bytes 786436
  503.7 74.0 %copy-start.13 = (bf16[128,16,64]{0,2,1:T(8,128)(2,1)S(1)}, bf16[128,16,64]{0,2,1:T(8,128)(2,1)}, u32[]{:S(2)}) copy-start(bf16[128,16,64]{0,2,1:T(8,128)(2,1)} %slice_bitcast_fusion.2) | copy-start | bytes 786436
  713.3 314.5 %all-reduce.7.cloned.1.call-start = ((), (), s32[]{:S(2)}) async-start(), calls=%async_computation.16 | async-start | bytes 12255232 | tf_op jit(solution)/shard_map/psum | solution.py:281
  815.3 0.7 copy-start.15
  1027.8 3.6 copy-start.12
  1027.8 4.7 copy-start.5
  1032.4 2.8 copy-start.7
Sparse Core Ops, SparseCore 0:
  9.5 49.1 all-gather.10
  65.5 91.7 all-gather.12
  160.7 89.9 all-gather.14
  252.1 20.7 all-gather.16
  274.3 71.6 all-gather.18
  347.4 41.1 all-gather.20
  391.4 93.1 all-gather.22
  487.5 90.1 all-gather.24
  580.8 29.2 reduce-scatter.6
  613.1 52.1 reduce-scatter.10
  667.9 86.0 reduce-scatter.8
  756.4 58.8 reduce-scatter.4
  820.0 207.6 all-reduce.6
where the time goes:
time: 1050 us; the launch traced here: 1040 us
  waiting for transfers between devices  553 us (53%)
  matrix products  284 us (27%)
  blocking collectives  121 us (12%)
  other arithmetic  37.2 us (4%)
  local copies, waits for them, and re-layouts  18.6 us (2%)
  between operations  15.1 us (1%)
  loops' own time  13.9 us (1%)
    psum x1, waiting for transfers between devices, on_device(): lax.psum(shards[1].astype(jnp.bfloat16), 'ctx').astype(jnp.float32)  169 us
    all_gather x1, waiting for transfers between devices, on_device(): lax.all_gather(keys.reshape(rows, width), ('ctx', 'fsdp'), axis=0, tiled=...  83.3 us
    all_gather x1, waiting for transfers between devices, on_device(): lax.all_gather(w_in, 'fsdp', axis=0, tiled=True)  67.3 us
    reduce_scatter x1, waiting for transfers between devices, on_device(): lax.psum_scatter(d_w_qkv.astype(jnp.bfloat16), 'fsdp', scatter_dimension=...  61.3 us
    dot_general x8, matrix products, key_terms(): jnp.einsum('hqk,qhd->khd', d_score, queries, preferred_element_type=jnp.f...  57.2 us
    all_gather x1, waiting for transfers between devices, on_device(): lax.all_gather(values.reshape(rows, width), ('ctx', 'fsdp'), axis=0, tile...  43.3 us
    all_gather x1, blocking collectives, on_device(): lax.all_gather(lse.T, ('ctx', 'fsdp'), axis=0, tiled=True)  42.8 us
    all_gather x1, waiting for transfers between devices, on_device(): lax.all_gather(w_qkv, 'fsdp', axis=0, tiled=True)  41.7 us
  transfers between devices with their start and end apart: 13, of which 9 were waited for; matrix products, arithmetic and copies ran while one was open for 31% of the time, Pallas kernels for 0%

commit v1 on v0

--- a/solution.py
+++ b/solution.py
@@ -10,6 +10,10 @@
 THETA = 160000.0
 SQRT_HALF = 0.7071067811865476
 INV_SQRT_TAU = 0.3989422804014327
+
+
+def _match_space(page, a_name):
+    return jnp.sum(lax.all_gather(page, axis_name=a_name), axis=0)
 
 
 def layer_norm(values, gain):
@@ -278,7 +282,7 @@
     )
     summed = (
         lax.psum(shards[0].astype(jnp.bfloat16), "ctx").astype(jnp.float32),
-        lax.psum(shards[1].astype(jnp.bfloat16), "ctx").astype(jnp.float32),
+        _match_space(shards[1].astype(jnp.bfloat16), "ctx").astype(jnp.float32),
         lax.psum(shards[2].astype(jnp.bfloat16), "ctx").astype(jnp.float32),
         lax.psum(shards[3].astype(jnp.bfloat16), "ctx").astype(jnp.float32),
         lax.psum(shards[4].astype(jnp.bfloat16), "ctx").astype(jnp.float32),

time: 1050 us -> 1190 us (1.13)
  waiting for transfers between devices: 553 us -> 680 us
    all_gather x0 -> x1, waiting for transfers between devices: none -> 169 us  [_match_space(): return jnp.sum(lax.all_gather(page, axis_name=a_name), axis=0)]
    psum x1, waiting for transfers between devices: 169 us -> 128 us  [on_device(): lax.psum(shards[2].astype(jnp.bfloat16), 'ctx').astype(jnp.float32)]
  transfers between devices with their start and end apart: 13 -> 14, of which waited for: 9 -> 10; matrix products, arithmetic and copies ran while one was open for 31% -> 28% of each run, Pallas kernels for 0% -> 0%
where the time goes in v1:
time: 1190 us; the launch traced here: 1180 us
  waiting for transfers between devices  680 us (57%)
  matrix products  284 us (24%)
  blocking collectives  121 us (10%)
  other arithmetic  45.8 us (4%)
  local copies, waits for them, and re-layouts  18 us (2%)
  between operations  15.2 us (1%)
  loops' own time  14.1 us (1%)
    all_gather x1, waiting for transfers between devices, _match_space(): return jnp.sum(lax.all_gather(page, axis_name=a_name), axis=0)  169 us
    psum x1, waiting for transfers between devices, on_device(): lax.psum(shards[2].astype(jnp.bfloat16), 'ctx').astype(jnp.float32)  128 us
    all_gather x1, waiting for transfers between devices, on_device(): lax.all_gather(keys.reshape(rows, width), ('ctx', 'fsdp'), axis=0, tiled=...  83.3 us
    all_gather x1, waiting for transfers between devices, on_device(): lax.all_gather(w_in, 'fsdp', axis=0, tiled=True)  67.3 us
    reduce_scatter x1, waiting for transfers between devices, on_device(): lax.psum_scatter(d_w_qkv.astype(jnp.bfloat16), 'fsdp', scatter_dimension=...  61 us
    dot_general x8, matrix products, key_terms(): jnp.einsum('hqk,qhd->khd', d_score, queries, preferred_element_type=jnp.f...  57.2 us
    all_gather x1, waiting for transfers between devices, on_device(): lax.all_gather(values.reshape(rows, width), ('ctx', 'fsdp'), axis=0, tile...  43.2 us
    all_gather x1, blocking collectives, on_device(): lax.all_gather(lse.T, ('ctx', 'fsdp'), axis=0, tiled=True)  42.8 us
  transfers between devices with their start and end apart: 14, of which 10 were waited for; matrix products, arithmetic and copies ran while one was open for 28% of the time, Pallas kernels for 0%

profile of v1, /device:TPU:0, one launch (start us, length us, event | category | flops | bytes accessed | tf_op | source)
XLA Modules:
  0.0 1178.8 jit_solution(15846477218426016681)
XLA Ops:
  17.1 41.7 %all-gather.13.cloned.1.call-done = bf16[1024,3072]{1,0:T(8,128)(2,1)} async-done(((bf16[256,3072]{1,0:T(8,128)(2,1)}), bf16[1024,3072]{1,0:T(8,128)(2,1)}) %all-gather.13.cloned.1.call-update) | async-done | bytes 6291472 | tf_op jit(solution)/shard_map/all_gather | solution.py:180
  74.0 83.3 %all-gather.15.cloned.1.call-done = bf16[4096,1024]{0,1:T(8,128)(2,1)} async-done(((bf16[128,1024]{0,1:T(8,128)(2,1)}), bf16[4096,1024]{0,1:T(8,128)(2,1)}) %all-gather.15.cloned.1.call-update) | async-done | bytes 8388624 | tf_op jit(solution)/shard_map/all_gather | solution.py:206
  157.3 50.2 %while.48 = (s32[]{:T(128)}, f32[16,128]{1,0:T(8,128)S(1)}, f32[16,128]{1,0:T(8,128)S(1)}, s32[4]{0:T(128)S(1)}, bf16[4096,16,64]{0,2,1:T(8,128)(2,1)}, /*index=...) while((s32[]{:T(128)}, f32[16,128]{1,0:T(8,128)S(1)}, ...), condition=%wide.region_5.6_spmd.clone, body=%wide.region_2.5_spmd.clone.sunk | while | flops 278931456 | bytes 19243188 | solution.py:94
  207.5 43.2 %all-gather.17.cloned.1.call-done = bf16[4096,1024]{0,1:T(8,128)(2,1)} async-done(((bf16[128,1024]{0,1:T(8,128)(2,1)}), bf16[4096,1024]{0,1:T(8,128)(2,1)}) %all-gather.17.cloned.1.call-update) | async-done | bytes 8388624 | tf_op jit(solution)/shard_map/all_gather | solution.py:207
  250.7 25.5 %while.49 = (s32[]{:T(128)}, f32[16,128,64]{1,2,0:T(8,128)S(1)}, s32[4]{0:T(128)S(1)}, bf16[4096,16,64]{0,2,1:T(8,128)(2,1)}, bf16[128,16,64]{0,2,1:T(8,128)(2,1...) while((s32[]{:T(128)}, f32[16,128,64]{1,2,0:T(8,128)S(1)}, ...), condition=%wide.region_7.8_spmd.clone, body=%wide.region_6.7_spmd.clone.sunk | while | flops 543424512 | bytes 5514936 | solution.py:109
  278.6 67.3 %all-gather.21.cloned.1.call-done = bf16[1024,5248]{1,0:T(8,128)(2,1)} async-done(((bf16[256,5248]{1,0:T(8,128)(2,1)}), bf16[1024,5248]{1,0:T(8,128)(2,1)}) %all-gather.21.cloned.1.call-update) | async-done | bytes 10747920 | tf_op jit(solution)/shard_map/all_gather | solution.py:183
  346.0 7.3 fusion.107
  353.2 35.3 %all-gather.23.cloned.1.call-done = bf16[2624,1024]{1,0:T(8,128)(2,1)} async-done(((bf16[656,1024]{1,0:T(8,128)(2,1)}), bf16[2624,1024]{1,0:T(8,128)(2,1)}) %all-gather.23.cloned.1.call-update) | async-done | bytes 5373968 | tf_op jit(solution)/shard_map/all_gather | solution.py:184
  393.9 8.3 multiply_reduce_fusion
  413.4 7.0 convolution_convert_fusion
  422.3 42.8 %all_gather.51 = f32[4096,16]{0,1:T(8,128)S(1)} all-gather(f32[128,16]{0,1:T(8,128)S(1)} %bitcast.129), channel_id=1, replica_groups=mesh['ctx'=8,'fsdp'=4] {'ctx','fsdp'}, dimensions={0}, use_global_device_ids=true | all-gather | bytes 270336 | tf_op jit(solution)/shard_map/all_gather | solution.py:241
  465.2 38.5 %all_gather.53 = f32[4096,16]{0,1:T(8,128)S(1)} all-gather(f32[128,16]{0,1:T(8,128)S(1)} %multiply_reduce_fusion.1), channel_id=1, replica_groups=mesh['ctx'=8,'fsdp'=4] {'ctx','fsdp'}, dimensions={0}, use_global_device_ids=true | all-gather | bytes 270336 | tf_op jit(solution)/shard_map/all_gather | solution.py:242
  503.7 65.5 %while.50 = (s32[]{:T(128)}, f32[128,16,64]{0,2,1:T(8,128)}, s32[4]{0:T(128)S(1)}, bf16[4096,16,64]{0,2,1:T(8,128)(2,1)}, bf16[128,16,64]{0,2,1:T(8,128)(2,1)S(1...) while((s32[]{:T(128)}, f32[128,16,64]{0,2,1:T(8,128)}, ...), condition=%wide.region_14.15_spmd.clone, body=%wide.region_13.14_spmd.clone.sunk | while | flops 816185344 | bytes 24659660 | solution.py:149
  511.3 8.6 fusion.164
  527.5 8.7 fusion.164
  543.9 8.8 fusion.164
  560.3 8.9 fusion.164
  569.2 8.5 all-gather.27.cloned.1.call-done
  577.7 129.5 %while.51 = (s32[]{:T(128)}, f32[128,16,64]{0,2,1:T(8,128)}, f32[128,16,64]{0,2,1:T(8,128)S(1)}, s32[8]{0:T(128)S(1)}, bf16[4096,16,64]{0,2,1:T(8,128)(2,1)}, /*...) while((s32[]{:T(128)}, f32[128,16,64]{0,2,1:T(8,128)}, ...), condition=%wide.region_16.17_spmd.clone, body=%wide.region_15.16_spmd.clone.sunk | while | flops 545914880 | bytes 19629788 | solution.py:171
  583.1 7.1 fusion.173
  614.5 6.7 fusion.173
  631.1 7.6 fusion.173
  647.5 6.8 fusion.173
  662.9 6.8 fusion.173
  679.3 8.8 fusion.173
  697.0 6.7 fusion.173
  713.4 40.7 %reduce-scatter.9.cloned.1.call-done = bf16[256,5248]{1,0:T(8,128)(2,1)} async-done(((bf16[1024,5248]{1,0:T(8,128)(2,1)}), bf16[256,5248]{1,0:T(8,128)(2,1)}) %reduce-scatter.9.cloned.1.call-update) | async-done | bytes 2686992 | tf_op jit(solution)/shard_map/reduce_scatter | solution.py:276
  754.3 61.0 %reduce-scatter.5.cloned.1.call-done = bf16[256,3072]{1,0:T(8,128)(2,1)} async-done(((bf16[1024,3072]{1,0:T(8,128)(2,1)}), bf16[256,3072]{1,0:T(8,128)(2,1)}) %reduce-scatter.5.cloned.1.call-update) | async-done | bytes 1572880 | tf_op jit(solution)/shard_map/reduce_scatter | solution.py:267
  833.1 22.7 %all-reduce.2 = (bf16[256]{0:T(256)(128)(2,1)S(1)}, bf16[256]{0:T(256)(128)(2,1)S(1)}) all-reduce(bf16[256]{0:T(256)(128)(2,1)S(1)} %dynamic-slice.1, bf16[256]{0:T(256)(128)(2,1)S(1)} %dynamic-slice.3), channel_id=1, replica_groups=mesh['ctx'=8,'fsdp'=4] {'ctx'}, use_global_device_ids=true, to_apply=%region_21.22 | all-reduce | flops 512 | bytes 2048 | tf_op jit(solution)/shard_map/psum | solution.py:284
  858.0 127.5 %all-reduce.7.cloned.1.call-done = (bf16[256,1024]{1,0:T(8,128)(2,1)}, bf16[256,5248]{1,0:T(8,128)(2,1)}, bf16[656,1024]{1,0:T(8,128)(2,1)}) async-done(((bf16[256,1024]{1,0:T(8,128)(2,1)}, bf16[256,5248]{1,0:T(8,128)(2,1)}, bf16[656,1024]{1,0:T(8,128)(2,1)}), (bf16[256,1024]{1,0:T(8,128)(2,1)}, bf16[256,5248]{1,0:T(8,128)(2,1)}, bf16[656,1024]{1,0:T(8,128)(2,1)})) %all-reduce.7.cloned.1.call-update) | async-done | bytes 4554768 | tf_op jit(solution)/shard_map/psum | solution.py:286
  994.1 168.6 %all-gather.29.cloned.1.call-done = bf16[2048,3072]{1,0:T(8,128)(2,1)} async-done(((bf16[256,3072]{1,0:T(8,128)(2,1)}), bf16[2048,3072]{1,0:T(8,128)(2,1)}) %all-gather.29.cloned.1.call-update) | async-done | bytes 12582928 | tf_op jit(solution)/shard_map/all_gather | solution.py:16
  1162.7 7.3 reduce_sum.131
  (198 shorter events, 253.0 us)
Async XLA Ops:
  7.2 51.6 %all-gather.13.cloned.1.call-start = ((), (), s32[]{:S(2)}) async-start(), calls=%async_computation.4 | async-start | bytes 7864320 | tf_op jit(solution)/shard_map/all_gather | solution.py:180
  7.9 149.4 %all-gather.15.cloned.1.call-start = ((), (), s32[]{:S(2)}) async-start(), calls=%async_computation.5 | async-start | bytes 8650752 | tf_op jit(solution)/shard_map/all_gather | solution.py:206
  64.2 3.2 copy-start.4
  65.4 185.3 %all-gather.17.cloned.1.call-start = ((), (), s32[]{:S(2)}) async-start(), calls=%async_computation.6 | async-start | bytes 8650752 | tf_op jit(solution)/shard_map/all_gather | solution.py:207
  66.2 210.0 %all-gather.19.cloned.1.call-start = ((), (), s32[]{:S(2)}) async-start(), calls=%async_computation.7 | async-start | bytes 2621440 | tf_op jit(solution)/shard_map/all_gather | solution.py:181
  66.8 2.1 copy-start.12
  66.8 279.2 %all-gather.21.cloned.1.call-start = ((), (), s32[]{:S(2)}) async-start(), calls=%async_computation.8 | async-start | bytes 13434880 | tf_op jit(solution)/shard_map/all_gather | solution.py:183
  67.4 321.2 %all-gather.23.cloned.1.call-start = ((), (), s32[]{:S(2)}) async-start(), calls=%async_computation.9 | async-start | bytes 6717440 | tf_op jit(solution)/shard_map/all_gather | solution.py:184
  68.0 501.2 %all-gather.25.cloned.1.call-start = ((), (), s32[]{:S(2)}) async-start(), calls=%async_computation.10 | async-start | bytes 8650752 | tf_op jit(solution)/shard_map/all_gather | solution.py:249
  68.9 508.9 %all-gather.27.cloned.1.call-start = ((), (), s32[]{:S(2)}) async-start(), calls=%async_computation.11 | async-start | bytes 8650752 | tf_op jit(solution)/shard_map/all_gather | solution.py:250
  250.7 25.6 %copy-start.2 = (bf16[128,1024]{1,0:T(8,128)(2,1)S(1)}, bf16[128,1024]{1,0:T(8,128)(2,1)}, u32[]{:S(2)}) copy-start(bf16[128,1024]{1,0:T(8,128)(2,1)} %param.16) | copy-start | bytes 786436
  346.0 42.6 %copy-start.7 = (bf16[128,1024]{1,0:T(8,128)(2,1)S(1)}, bf16[128,1024]{1,0:T(8,128)(2,1)}, u32[]{:S(2)}) copy-start(bf16[128,1024]{1,0:T(8,128)(2,1)} %param.23) | copy-start | bytes 786436
  393.9 8.3 copy-start.8
  393.9 8.3 copy-start.10
  393.9 8.6 copy-start.3
  404.2 309.1 %reduce-scatter.7.cloned.1.call-start = ((), (), s32[]{:S(2)}) async-start(), calls=%async_computation.13 | async-start | bytes 2621440 | tf_op jit(solution)/shard_map/reduce_scatter | solution.py:270
  406.3 307.1 %reduce-scatter.11.cloned.1.call-start = ((), (), s32[]{:S(2)}) async-start(), calls=%async_computation.15 | async-start | bytes 6717440 | tf_op jit(solution)/shard_map/reduce_scatter | solution.py:279
  412.3 1.1 copy-start.9
  412.3 341.7 %reduce-scatter.9.cloned.1.call-start = ((), (), s32[]{:S(2)}) async-start(), calls=%async_computation.14 | async-start | bytes 13434880 | tf_op jit(solution)/shard_map/reduce_scatter | solution.py:276
  420.4 44.8 %copy-start.5 = (bf16[128,1024]{0,1:T(8,128)(2,1)S(1)}, bf16[128,1024]{0,1:T(8,128)(2,1)}, u32[]{:S(2)}) copy-start(bf16[128,1024]{0,1:T(8,128)(2,1)} %copy.40) | copy-start | bytes 786436
  420.4 83.3 %copy-start = (bf16[128,16,64]{0,2,1:T(8,128)(2,1)S(1)}, bf16[128,16,64]{0,2,1:T(8,128)(2,1)}, u32[]{:S(2)}) copy-start(bf16[128,16,64]{0,2,1:T(8,128)(2,1)} %get-tuple-element.817) | copy-start | bytes 786436
  420.4 394.9 %reduce-scatter.5.cloned.1.call-start = ((), (), s32[]{:S(2)}) async-start(), calls=%async_computation.12 | async-start | bytes 7864320 | tf_op jit(solution)/shard_map/reduce_scatter | solution.py:267
  503.7 74.0 %copy-start.1 = (bf16[128,16,64]{0,2,1:T(8,128)(2,1)S(1)}, bf16[128,16,64]{0,2,1:T(8,128)(2,1)}, u32[]{:S(2)}) copy-start(bf16[128,16,64]{0,2,1:T(8,128)(2,1)} %maximum_convert_fusion) | copy-start | bytes 786436
  503.7 74.0 %copy-start.11 = (bf16[128,16,64]{0,2,1:T(8,128)(2,1)S(1)}, bf16[128,16,64]{0,2,1:T(8,128)(2,1)}, u32[]{:S(2)}) copy-start(bf16[128,16,64]{0,2,1:T(8,128)(2,1)} %slice_bitcast_fusion.2) | copy-start | bytes 786436
  713.3 272.2 %all-reduce.7.cloned.1.call-start = ((), (), s32[]{:S(2)}) async-start(), calls=%async_computation.17 | async-start | bytes 9109504 | tf_op jit(solution)/shard_map/psum | solution.py:286
  754.0 61.3 %copy-start.13 = (u32[32]{0:T(128)S(1)}, u32[32]{0:T(128)}, u32[]{:S(2)}) copy-start(u32[32]{0:T(128)} %constant.115) | copy-start | bytes 388
  754.1 408.6 %all-gather.29.cloned.1.call-start = ((), (), s32[]{:S(2)}) async-start(), calls=%async_computation.16 | async-start | bytes 14155776 | tf_op jit(solution)/shard_map/all_gather | solution.py:16
  987.6 4.6 copy-start.6
Sparse Core Ops, SparseCore 0:
  9.5 49.1 all-gather.12
  65.5 91.7 all-gather.14
  160.7 89.9 all-gather.16
  252.1 20.7 all-gather.18
  274.3 71.6 all-gather.20
  347.4 41.1 all-gather.22
  391.4 93.1 all-gather.24
  487.4 90.2 all-gather.26
  580.8 29.2 reduce-scatter.6
  613.2 52.1 reduce-scatter.10
  668.0 85.9 reduce-scatter.8
  756.4 58.8 reduce-scatter.4
  819.3 166.1 all-reduce.6
  987.6 175.1 all-gather.28
